TPU v7x, 32 devices: a whole 2x2x4 slice. The times are simulated.
32 devices in a mesh: tm: 4 (over y, x), space: 8 (over z, core).
Axes of the slice: x: 2, y: 2, z: 4, core: 2. Of those that a mesh axis runs over, the one named last changes fastest.
Arguments:
- vectors: float32 [4, 2, 3, 64, 2048], P('tm', None, None, None, 'space'), may hold values from -6 to 6
- perambulators: float32 [4, 16, 2, 4096], P('tm'), may hold values from -0.75 to 0.75
- shift_steps: int32 [4], P('tm'), may hold values from 1 to 3, as said below
- spin_choice: int32 [4, 3], replicated, may hold values from 0 to 15
Outputs:
- elementals: float32 [4, 64, 2, 4096], P('tm', 'space')
- correlator: float32 [4, 4, 2], P('tm')
Inputs may be any that keep to these rules, and one draw needn't show every extreme that they name: `shift_steps`: every distance from 1 to 3 is taken by at least one source timeslice. `spin_choice`: each entry is alpha 4 + beta for a pair of spin indices.
All inputs are finite; a program needn't handle non-finite values.
Results may differ from a plain program's by a relative error of at most 0.0003.
Values sent between devices are 32-bit elements; how exact they have to be, the bound alone decides.
A program may use at most 64 MiB of HBM per device.

v0:
```python
import math

import jax
import jax.numpy as jnp
from jax import lax
from jax.sharding import PartitionSpec as P

exact_mode = lax.Precision.HIGHEST


def complex_product(left_re, left_im, right_re, right_im):
    return (left_re * right_re - left_im * right_im, left_re * right_im + left_im * right_re)


def rotate(values, places):
    return jnp.concatenate([values[places:], values[:places]], axis=0)


def contract_first(left, right):
    return lax.dot_general(left, right, (((0,), (0,)), ((), ())), precision=exact_mode)


def inner_rows(left, right):
    return lax.dot_general(left, right, (((1,), (1,)), ((), ())), precision=exact_mode)


def complex_einsum(form, left, right):
    first = jnp.einsum(form, left[0], right[0], precision=exact_mode) - jnp.einsum(
        form, left[1], right[1], precision=exact_mode
    )
    second = jnp.einsum(form, left[0], right[1], precision=exact_mode) + jnp.einsum(
        form, left[1], right[0], precision=exact_mode
    )
    return (first, second)


def elemental_rows(vec_re, vec_im, lead_re, lead_im, first_row, row_count, factor):
    sites = vec_re.shape[1]
    nvec = vec_re.shape[2]
    block = math.gcd(row_count, 4)

    def one_block(index):
        offset = first_row + index * block
        part_re = lax.dynamic_slice_in_dim(vec_re, offset, block, 2)[:, :, :, None]
        part_im = lax.dynamic_slice_in_dim(vec_im, offset, block, 2)[:, :, :, None]
        full_re = vec_re[:, :, None, :]
        full_im = vec_im[:, :, None, :]
        one_re, one_im = complex_product(
            rotate(part_re, 1), rotate(part_im, 1), rotate(full_re, 2), rotate(full_im, 2)
        )
        two_re, two_im = complex_product(
            rotate(part_re, 2), rotate(part_im, 2), rotate(full_re, 1), rotate(full_im, 1)
        )
        cross_re = (one_re - two_re).reshape(3 * sites, block * nvec)
        cross_im = (one_im - two_im).reshape(3 * sites, block * nvec)
        out_re = contract_first(lead_re, cross_re) - contract_first(lead_im, cross_im)
        out_im = contract_first(lead_re, cross_im) + contract_first(lead_im, cross_re)
        stacked = jnp.stack([out_re, out_im], 0).reshape(2, nvec, block, nvec)
        return jnp.transpose(stacked, (2, 0, 1, 3)).reshape(block, 2, nvec * nvec) * factor

    result = lax.map(one_block, jnp.arange(row_count // block, dtype=jnp.int32))
    return result.reshape(row_count, 2, nvec * nvec)


def transform_rows(own, mats, nvec):
    combos = mats.shape[0]
    row_count = own.shape[0]
    elem = (own[:, 0].reshape(row_count, nvec, nvec), own[:, 1].reshape(row_count, nvec, nvec))
    first_mat = (
        mats[:, 0, 0].reshape(combos, nvec, nvec),
        mats[:, 0, 1].reshape(combos, nvec, nvec),
    )
    third_mat = (
        mats[:, 2, 0].reshape(combos, nvec, nvec),
        mats[:, 2, 1].reshape(combos, nvec, nvec),
    )
    half = complex_einsum("jik,slk->sjil", elem, third_mat)
    done = complex_einsum("smi,sjil->sjml", first_mat, half)
    return (
        done[0].reshape(combos * row_count, nvec * nvec),
        done[1].reshape(combos * row_count, nvec * nvec),
    )


def pair_sum(sink_rows, trans_re, trans_im, mid_re, mid_im):
    combos = mid_re.shape[0]
    sink_count = sink_rows.shape[0]
    own_count = mid_re.shape[2]
    sink_re = sink_rows[:, 0]
    sink_im = sink_rows[:, 1]
    inner_re = (inner_rows(sink_re, trans_re) + inner_rows(sink_im, trans_im)).reshape(
        sink_count, combos, own_count
    )
    inner_im = (inner_rows(sink_re, trans_im) - inner_rows(sink_im, trans_re)).reshape(
        sink_count, combos, own_count
    )
    total_re = jnp.einsum("srj,rsj->s", mid_re, inner_re, precision=exact_mode) - jnp.einsum(
        "srj,rsj->s", mid_im, inner_im, precision=exact_mode
    )
    total_im = jnp.einsum("srj,rsj->s", mid_re, inner_im, precision=exact_mode) + jnp.einsum(
        "srj,rsj->s", mid_im, inner_re, precision=exact_mode
    )
    return jnp.stack([total_re, total_im], -1)


def shards(vectors, perambulators, shift_steps, spin_choice):
    local_vec = vectors[0]
    nvec = local_vec.shape[2]
    sites = local_vec.shape[3]
    space_count = lax.axis_size("space")
    time_count = lax.axis_size("tm")
    vec_re = jnp.transpose(local_vec[0], (0, 2, 1))
    vec_im = jnp.transpose(local_vec[1], (0, 2, 1))
    lead_re = vec_re.reshape(3 * sites, nvec)
    lead_im = vec_im.reshape(3 * sites, nvec)
    factor = 1.0 / math.sqrt(24.0 * sites * space_count)
    corr_factor = 0.25 / (nvec * math.sqrt(nvec))
    own_count = nvec // space_count
    own_first = lax.axis_index("space") * own_count
    summed = lax.psum(elemental_rows(vec_re, vec_im, lead_re, lead_im, 0, nvec, factor), "space")
    own = lax.dynamic_slice_in_dim(summed, own_first, own_count, 0)
    every_time = lax.all_gather(own[None], "tm", axis=0, tiled=True)
    target = (lax.axis_index("tm") + shift_steps[0]) % time_count
    sink = lax.dynamic_index_in_dim(every_time, target, 0, keepdims=False)
    combos = spin_choice.shape[0]
    spin_pairs = perambulators.shape[1]
    one_hot = (
        spin_choice[:, :, None] == jnp.arange(spin_pairs, dtype=jnp.int32)[None, None, :]
    ).astype(jnp.float32)
    mats = jnp.einsum("sqm,mcf->sqcf", one_hot, perambulators[0], precision=exact_mode)
    trans_re, trans_im = transform_rows(own, mats, nvec)
    mid_re = lax.dynamic_slice_in_dim(
        mats[:, 1, 0].reshape(combos, nvec, nvec), own_first, own_count, 2
    )
    mid_im = lax.dynamic_slice_in_dim(
        mats[:, 1, 1].reshape(combos, nvec, nvec), own_first, own_count, 2
    )
    sink_rows = lax.all_gather(sink, "space", axis=0, tiled=True)
    partial_corr = pair_sum(sink_rows, trans_re, trans_im, mid_re, mid_im)
    correlator = lax.psum(partial_corr, "space") * corr_factor
    return (own[None], correlator[None])


def solution(mesh):
    placed = (P("tm", None, None, None, "space"), P("tm", None, None, None), P("tm"), P())
    return jax.shard_map(
        shards,
        mesh=mesh,
        in_specs=placed,
        out_specs=(P("tm", "space", None, None), P("tm", None, None)),
        check_vma=False,
    )
```

profile of v0, /device:TPU:0, one launch (start us, length us, event | category | flops | bytes accessed | tf_op | source)
XLA Modules:
  0.0 342.0 jit_solution(15728689861665589250)
XLA Ops:
  7.2 1.0 fusion.30
  8.3 1.1 copy_bitcast_fusion
  9.3 1.1 slice_bitcast_fusion.7
  10.5 1.1 slice_bitcast_fusion.11
  11.6 1.1 slice_bitcast_fusion.6
  12.8 1.1 slice_bitcast_fusion.10
  13.9 1.1 copy.20
  15.0 1.1 copy.21
  16.7 163.7 %while.11 = (s32[]{:T(128)}, f32[16,4,2,4096]{3,2,1,0:T(2,128)}, s32[16]{0:T(128)S(1)}, f32[3,256,64]{1,0,2:T(4,128)}, f32[3,256,1,64]{1,0,3,2:T(4,128)S(1)}, /*...) while((s32[]{:T(128)}, f32[16,4,2,4096]{3,2,1,0:T(2,128)}, ...), condition=%wide.region_1.2_spmd, body=%wide.region_0.1_spmd.sunk | while | flops 606842880 | bytes 11387647 | solution.py:61
  19.8 1.0 subtract_subtract_fusion.2
  21.9 1.4 fusion.77
  30.0 1.0 subtract_subtract_fusion.2
  32.1 1.4 fusion.77
  40.3 1.0 subtract_subtract_fusion.2
  42.4 1.4 fusion.77
  50.5 1.0 subtract_subtract_fusion.2
  52.6 1.4 fusion.77
  60.7 1.0 subtract_subtract_fusion.2
  62.8 1.4 fusion.77
  71.0 1.0 subtract_subtract_fusion.2
  73.1 1.4 fusion.77
  81.2 1.0 subtract_subtract_fusion.2
  83.3 1.4 fusion.77
  91.4 1.0 subtract_subtract_fusion.2
  93.5 1.4 fusion.77
  101.7 1.0 subtract_subtract_fusion.2
  103.8 1.4 fusion.77
  111.9 1.0 subtract_subtract_fusion.2
  114.0 1.4 fusion.77
  122.1 1.0 subtract_subtract_fusion.2
  124.2 1.4 fusion.77
  132.3 1.0 subtract_subtract_fusion.2
  134.4 1.4 fusion.77
  142.6 1.0 subtract_subtract_fusion.2
  144.7 1.4 fusion.77
  152.8 1.0 subtract_subtract_fusion.2
  154.9 1.4 fusion.77
  163.0 1.0 subtract_subtract_fusion.2
  165.1 1.4 fusion.77
  173.2 1.0 subtract_subtract_fusion.2
  175.3 1.4 fusion.77
  180.4 4.1 %copy.22 = f32[64,2,4096]{2,0,1:T(8,128)} copy(f32[64,2,4096]{2,1,0:T(2,128)} %bitcast.264) | data formatting | bytes 4194304 | tf_op jit(solution)/shard_map/reshape | solution.py:62
  184.6 67.9 %all-reduce.2.cloned.1.call-done = f32[64,2,4096]{2,0,1:T(8,128)} async-done(((f32[64,2,4096]{2,0,1:T(8,128)}), f32[64,2,4096]{2,0,1:T(8,128)}) %all-reduce.2.cloned.1.call-update) | async-done | bytes 2097168 | tf_op jit(solution)/shard_map/psum | solution.py:120
  252.5 1.7 constant_dynamic-slice_fusion.3
  255.9 25.2 %all-gather.5.cloned.1.call-done = f32[32,2,4096]{2,0,1:T(8,128)} async-done(((f32[8,2,4096]{2,0,1:T(8,128)}), f32[32,2,4096]{2,0,1:T(8,128)}) %all-gather.5.cloned.1.call-update) | async-done | bytes 1048592 | tf_op jit(solution)/shard_map/all_gather | solution.py:122
  281.1 1.7 constant_dynamic-slice_fusion.2
  283.9 1.0 constant_dynamic-slice_fusion
  285.1 1.0 fusion.20
  286.1 1.0 fusion.24
  287.1 1.0 fusion.5
  288.1 1.0 fusion.16
  289.2 1.0 fusion.6
  290.2 1.0 fusion.3
  291.2 1.3 copy.27
  292.6 1.6 reshape.145
  294.1 1.0 fusion.18
  295.2 1.0 fusion.4
  296.2 1.3 copy.26
  297.5 1.6 reshape.144
  299.1 12.9 %all-gather.7.cloned.1.call-done = f32[1,64,2,4096]{3,1,0,2:T(8,128)} async-done(((f32[1,8,2,4096]{3,1,0,2:T(8,128)}), f32[1,64,2,4096]{3,1,0,2:T(8,128)}) %all-gather.7.cloned.1.call-update) | async-done | bytes 2097168 | tf_op jit(solution)/shard_map/all_gather | solution.py:138
  312.1 2.3 fusion.9
  314.4 2.2 fusion.10
  317.6 1.1 multiply_reduce_fusion.2
  319.6 15.2 %psum.15 = f32[4,2]{0,1:T(2,128)S(1)} all-reduce(f32[4,2]{0,1:T(2,128)S(1)} %pad_maximum_fusion.4), channel_id=1, replica_groups=mesh['tm'=4,'space'=8] {'space'}, use_global_device_ids=true, to_apply=%region_3.4 | all-reduce | flops 8 | bytes 64 | tf_op jit(solution)/shard_map/psum | solution.py:140
  (328 shorter events, 118.0 us)
Async XLA Ops:
  7.2 245.4 %all-reduce.2.cloned.1.call-start = ((), (), s32[]{:S(2)}) async-start(), calls=%async_computation | async-start | bytes 4194304 | tf_op jit(solution)/shard_map/psum | solution.py:120
  184.5 70.6 %copy-start.3 = (s32[4,3]{1,0:T(4,128)S(1)}, s32[4,3]{1,0:T(4,128)}, u32[]{:S(2)}) copy-start(s32[4,3]{1,0:T(4,128)} %param.9) | copy-start | bytes 148
  184.5 70.7 %copy-start.2 = (f32[1,16,2,4096]{3,2,1,0:T(2,128)S(1)}, f32[1,16,2,4096]{3,2,1,0:T(2,128)}, u32[]{:S(2)}) copy-start(f32[1,16,2,4096]{3,2,1,0:T(2,128)} %param.7) | copy-start | bytes 1572868
  184.5 96.6 %all-gather.5.cloned.1.call-start = ((), (), s32[]{:S(2)}) async-start(), calls=%async_computation.1 | async-start | bytes 1310720 | tf_op jit(solution)/shard_map/all_gather | solution.py:122
  254.2 57.9 %all-gather.7.cloned.1.call-start = ((), (), s32[]{:S(2)}) async-start(), calls=%async_computation.2 | async-start | bytes 2359296 | tf_op jit(solution)/shard_map/all_gather | solution.py:138
  312.1 4.5 %copy-start = (f32[1,64,2,4096]{3,1,0,2:T(8,128)S(1)}, f32[1,64,2,4096]{3,1,0,2:T(8,128)}, u32[]{:S(2)}) copy-start(f32[1,64,2,4096]{3,1,0,2:T(8,128)} %all-gather.7.cloned.1.call-done) | copy-start | bytes 6291460
  314.4 4.3 %copy-start.1 = (f32[8,2,4096]{2,0,1:T(8,128)S(1)}, f32[8,2,4096]{2,0,1:T(8,128)}, u32[]{:S(2)}) copy-start(f32[8,2,4096]{2,0,1:T(8,128)} %constant_dynamic-slice_fusion.3) | copy-start | bytes 786436
Sparse Core Ops, SparseCore 0:
  184.6 67.8 all-reduce.1
  254.9 26.0 all-gather.4
  282.9 29.1 all-gather.6
where the time goes:
time: 347 us; the launch traced here: 342 us
  waiting for transfers between devices  106 us (31%)
  local copies, waits for them, and re-layouts  97.5 us (28%)
  matrix products  76.3 us (22%)
  other arithmetic  18.9 us (5%)
  blocking collectives  15.2 us (4%)
  between operations  14.7 us (4%)
  loops' own time  12.9 us (4%)
    psum x1, waiting for transfers between devices, shards(): lax.psum(elemental_rows(vec_re, vec_im, lead_re, lead_im, 0, nvec, factor...  67.9 us
    dot_general x64, matrix products, contract_first(): lax.dot_general(left, right, (((0,), (0,)), ((), ())), precision=exact_mode)  60.9 us
    slice x36, local copies, waits for them, and re-layouts, rotate(): return jnp.concatenate([values[places:], values[:places]], axis=0)  30.9 us
    all_gather x1, waiting for transfers between devices, shards(): every_time = lax.all_gather(own[None], 'tm', axis=0, tiled=True)  25.2 us
    another operation x32, local copies, waits for them, and re-layouts, one_block(): stacked = jnp.stack([out_re, out_im], 0).reshape(2, nvec, block, nvec)  17 us
    sub x16, other arithmetic, one_block(): cross_re = (one_re - two_re).reshape(3 * sites, block * nvec)  15.5 us
    psum x1, blocking collectives, shards(): correlator = lax.psum(partial_corr, 'space') * corr_factor  15.2 us
    all_gather x1, waiting for transfers between devices, shards(): sink_rows = lax.all_gather(sink, 'space', axis=0, tiled=True)  12.9 us
  transfers between devices with their start and end apart: 3, of which 3 were waited for; matrix products, arithmetic and copies ran while one was open for 5% of the time, Pallas kernels for 0%

commit v1 on v0

v1 whole, which is shorter than its diff:
```python
import functools
import math

import jax
import jax.numpy as jnp
from jax import lax
from jax.experimental import pallas as pl
from jax.experimental.pallas import tpu as pltpu
from jax.sharding import PartitionSpec as P

MESH = pl.DeviceIdType.MESH
VM = pl.BlockSpec(memory_space=pltpu.VMEM)
exact_mode = lax.Precision.HIGHEST
NT_DIMS = (((1,), (1,)), ((), ()))


def halves(x):
    top = x.astype(jnp.bfloat16)
    return top, (x - top.astype(jnp.float32)).astype(jnp.bfloat16)


def at_space(index):
    return (lax.axis_index("tm"), index)


def elementals_kernel(
    n, times, scale, v_ref, own_ref, full_ref, sink_ref,
    lead, d_hi, d_lo, keep, give, pair_in, chip_in,
    pair_send, pair_recv, chip_send, chip_recv,
    own_send, own_recv, fwd_send, fwd_recv, tm_send, tm_recv,
):
    me = lax.axis_index("space")
    tm = lax.axis_index("tm")
    chips = n // 2
    chip = me // 2
    core = me % 2
    mate = chip * 2 + 1 - core
    nvec = v_ref.shape[2]
    sites = v_ref.shape[3]
    own = nvec // n
    half = nvec // 2
    lanes = 2 * nvec
    group = 16 // own

    barrier = pltpu.get_barrier_semaphore()
    pl.semaphore_signal(barrier, inc=1, device_id=(tm, mate), device_id_type=MESH)
    for r in range(1, chips):
        pl.semaphore_signal(
            barrier, inc=1, device_id=(tm, (chip + r) % chips * 2 + core), device_id_type=MESH
        )
    for r in range(1, times):
        pl.semaphore_signal(
            barrier, inc=1, device_id=((tm + r) % times, me), device_id_type=MESH
        )
    pl.semaphore_wait(barrier, 1 + chips - 1 + times - 1)

    for kind in range(2):
        for a in range(3):
            re = v_ref[0, a]
            im = v_ref[1, a]
            if kind == 1:
                re = jnp.concatenate([re[half:], re[:half]], axis=0)
                im = jnp.concatenate([im[half:], im[:half]], axis=0)
            re_hi, re_lo = halves(re)
            im_hi, im_lo = halves(im)
            first = pl.ds(a * sites, sites)
            second = pl.ds((3 + a) * sites, sites)
            lead[kind, 0:nvec, first] = re_hi
            lead[kind, 0:nvec, second] = -im_hi
            lead[kind, nvec:lanes, first] = im_hi
            lead[kind, nvec:lanes, second] = re_hi
            lead[kind, lanes:lanes + nvec, first] = re_lo
            lead[kind, lanes:lanes + nvec, second] = -im_lo
            lead[kind, lanes + nvec:2 * lanes, first] = im_lo
            lead[kind, lanes + nvec:2 * lanes, second] = re_lo

    rows = half * own
    row_of = lax.broadcasted_iota(jnp.int32, (rows, lanes), 0) // own
    place = lax.broadcasted_iota(jnp.int32, (rows, lanes), 1) % nvec
    later = jnp.logical_or(place < half, place - half < row_of)

    def block(dest, out_ref):
        start = pl.multiple_of(dest * own, own)

        def rows_of(c, a):
            if own % 8 == 0:
                return v_ref[c, a, pl.ds(start, own), :]
            single = [v_ref[c, a, pl.ds(start + r, 1), :] for r in range(own)]
            return jnp.concatenate(single, axis=0)

        mine = [[rows_of(c, a) for a in range(3)] for c in range(2)]

        def fill(step, carry):
            base = step * group
            for side in range(2):
                got = []
                for g in range(group):
                    k = side * half + base + g
                    other = [[v_ref[c, a, pl.ds(k, 1), :] for a in range(3)] for c in range(2)]
                    cross = []
                    for a in range(3):
                        b, d = (a + 1) % 3, (a + 2) % 3
                        cross.append(
                            mine[0][b] * other[0][d] - mine[1][b] * other[1][d]
                            - (mine[0][d] * other[0][b] - mine[1][d] * other[1][b])
                        )
                    for a in range(3):
                        b, d = (a + 1) % 3, (a + 2) % 3
                        cross.append(
                            mine[0][b] * other[1][d] + mine[1][b] * other[0][d]
                            - (mine[0][d] * other[1][b] + mine[1][d] * other[0][b])
                        )
                    got.append(cross)
                at = pl.ds(pl.multiple_of(base * own, 16), 16)
                for m in range(6):
                    hi, lo = halves(jnp.concatenate([g[m] for g in got], axis=0))
                    d_hi[side, at, m * sites:(m + 1) * sites] = hi
                    d_lo[side, at, m * sites:(m + 1) * sites] = lo
            return carry

        lax.fori_loop(0, half // group, fill, 0)
        sums = []
        for side in range(2):
            kind = 1 - side
            both = lax.dot_general(
                d_hi[side], lead[kind], NT_DIMS, preferred_element_type=jnp.float32
            )
            rest = lax.dot_general(
                d_lo[side], lead[kind, 0:lanes], NT_DIMS, preferred_element_type=jnp.float32
            )
            sums.append(both[:, :lanes] + (both[:, lanes:] + rest))
        out_ref[...] = jnp.where(later, sums[1], sums[0])

    def pair_copy(s):
        return pltpu.make_async_remote_copy(
            give.at[s], pair_in.at[s], pair_send.at[s], pair_recv.at[s],
            device_id=(tm, mate), device_id_type=MESH,
        )

    def chip_copy(s):
        return pltpu.make_async_remote_copy(
            keep.at[s], chip_in.at[s], chip_send.at[s], chip_recv.at[s],
            device_id=(tm, (chip + 1 + s) % chips * 2 + core), device_id_type=MESH,
        )

    def one_chip(s, carry):
        z = (chip + 1 + s) % chips
        block(z * 2 + 1 - core, give.at[s])
        pair_copy(s).start()
        block(z * 2 + core, keep.at[s])
        pair_copy(s).wait_recv()
        keep[s] = keep[s] + pair_in[s]

        @pl.when(s < chips - 1)
        def _():
            chip_copy(s).start()

        return carry

    lax.fori_loop(0, chips, one_chip, 0)
    total = keep[chips - 1]
    for s in range(chips - 1):
        chip_copy(s).wait_recv()
        total = total + chip_in[s]
    own_ref[...] = total * scale

    def tm_copy(r):
        return pltpu.make_async_remote_copy(
            own_ref, sink_ref.at[r - 1], tm_send.at[r - 1], tm_recv.at[r - 1],
            device_id=((tm + r) % times, me), device_id_type=MESH,
        )

    def own_copy(r):
        target = mate if r == 0 else (chip + r) % chips * 2 + core
        return pltpu.make_async_remote_copy(
            own_ref, full_ref.at[me], own_send.at[r], own_recv.at[r],
            device_id=(tm, target), device_id_type=MESH,
        )

    def forward(r):
        slot = (chip + chips - r) % chips * 2 + core
        return pltpu.make_async_remote_copy(
            full_ref.at[slot], full_ref.at[slot], fwd_send.at[r - 1], fwd_recv.at[r - 1],
            device_id=(tm, mate), device_id_type=MESH,
        )

    for r in range(1, chips):
        own_copy(r).start()
    for r in range(1, times):
        tm_copy(r).start()
    own_copy(0).start()
    full_ref[me] = own_ref[...]
    for r in range(1, chips):
        own_copy(r).wait_recv()
        forward(r).start()
    for s in range(chips):
        pair_copy(s).wait_send()
    for s in range(chips - 1):
        chip_copy(s).wait_send()
    for r in range(1, times):
        tm_copy(r).wait()
    own_copy(0).wait()
    for r in range(1, chips):
        own_copy(r).wait_send()
        forward(r).wait()


def elementals(vec, n, times, scale):
    _, _, nvec, sites = vec.shape
    own, half = nvec // n, nvec // 2
    chips = n // 2
    tile = (half * own, 2 * nvec)
    f32 = jnp.float32
    dma = pltpu.SemaphoreType.DMA
    return pl.pallas_call(
        functools.partial(elementals_kernel, n, times, scale),
        out_shape=(
            jax.ShapeDtypeStruct(tile, f32),
            jax.ShapeDtypeStruct((n,) + tile, f32),
            jax.ShapeDtypeStruct((times - 1,) + tile, f32),
        ),
        in_specs=[VM],
        out_specs=(VM, VM, VM),
        scratch_shapes=[
            pltpu.VMEM((2, 4 * nvec, 6 * sites), jnp.bfloat16),
            pltpu.VMEM((2, half * own, 6 * sites), jnp.bfloat16),
            pltpu.VMEM((2, half * own, 6 * sites), jnp.bfloat16),
            pltpu.VMEM((chips,) + tile, f32),
            pltpu.VMEM((chips,) + tile, f32),
            pltpu.VMEM((chips,) + tile, f32),
            pltpu.VMEM((chips - 1,) + tile, f32),
            dma((chips,)), dma((chips,)),
            dma((chips - 1,)), dma((chips - 1,)),
            dma((chips,)), dma((chips,)),
            dma((chips - 1,)), dma((chips - 1,)),
            dma((times - 1,)), dma((times - 1,)),
        ],
        compiler_params=pltpu.CompilerParams(
            collective_id=0, has_side_effects=True, vmem_limit_bytes=60 * 1024 * 1024
        ),
        name="elementals",
    )(vec)


def sum_kernel(n, x_ref, o_ref, box, send, recv):
    me = lax.axis_index("space")
    tm = lax.axis_index("tm")
    barrier = pltpu.get_barrier_semaphore()
    for r in range(1, n):
        pl.semaphore_signal(barrier, inc=1, device_id=(tm, (me + r) % n), device_id_type=MESH)
    pl.semaphore_wait(barrier, n - 1)

    def copy(r):
        return pltpu.make_async_remote_copy(
            x_ref, box.at[r - 1], send.at[r - 1], recv.at[r - 1],
            device_id=(tm, (me + r) % n), device_id_type=MESH,
        )

    for r in range(1, n):
        copy(r).start()
    total = x_ref[...]
    for r in range(1, n):
        copy(r).wait_recv()
        total = total + box[r - 1]
    o_ref[...] = total
    for r in range(1, n):
        copy(r).wait_send()


def sum_space(x, n):
    dma = pltpu.SemaphoreType.DMA
    return pl.pallas_call(
        functools.partial(sum_kernel, n),
        out_shape=jax.ShapeDtypeStruct(x.shape, x.dtype),
        in_specs=[VM],
        out_specs=VM,
        scratch_shapes=[
            pltpu.VMEM((n - 1,) + x.shape, x.dtype), dma((n - 1,)), dma((n - 1,)),
        ],
        compiler_params=pltpu.CompilerParams(collective_id=1, has_side_effects=True),
        name="sum_space",
    )(x)


def unpack(packed):
    half, count, lanes = packed.shape
    nvec = lanes // 2
    rows = jnp.transpose(packed.reshape(half, count, 2, nvec), (1, 2, 0, 3))
    low_left, mixed = rows[..., :half], rows[..., half:]
    upper = jnp.triu(mixed, 1)
    lower = jnp.tril(mixed, -1)
    flip = lambda x: jnp.swapaxes(x, -1, -2)
    top = jnp.concatenate([upper - flip(upper), -flip(low_left)], axis=-1)
    bottom = jnp.concatenate([low_left, lower - flip(lower)], axis=-1)
    return -jnp.concatenate([top, bottom], axis=-2)


def complex_einsum(form, left, right):
    def dot(a, b):
        return jnp.einsum(form, a, b, precision=exact_mode)

    return (
        dot(left[0], right[0]) - dot(left[1], right[1]),
        dot(left[0], right[1]) + dot(left[1], right[0]),
    )


def shards(vectors, perambulators, shift_steps, spin_choice):
    vec = vectors[0]
    nvec = vec.shape[2]
    sites = vec.shape[3]
    n = lax.axis_size("space")
    times = lax.axis_size("tm")
    own = nvec // n
    scale = 1.0 / math.sqrt(24.0 * sites * n)
    corr_scale = 0.25 / (nvec * math.sqrt(nvec))
    mine, full, sinks = elementals(vec, n, times, scale)
    packed = (nvec // 2, own, 2 * nvec)
    out = unpack(mine.reshape(packed)).reshape(own, 2, nvec * nvec)
    chosen = lax.dynamic_index_in_dim(sinks, times - shift_steps[0] - 1, 0, keepdims=False)
    sink = unpack(chosen.reshape(packed))
    full = jnp.transpose(full.reshape((n,) + packed), (1, 0, 2, 3))
    whole = unpack(full.reshape(nvec // 2, nvec, 2 * nvec))
    mats = perambulators[0][spin_choice].reshape(spin_choice.shape + (2, nvec, nvec))
    first = lax.axis_index("space") * own
    mid = lax.dynamic_slice_in_dim(mats[:, 1], first, own, 2)
    two = complex_einsum("jml,slk->sjmk", (sink[:, 0], -sink[:, 1]), (mats[:, 2, 0], mats[:, 2, 1]))
    one = complex_einsum("sjmk,smi->sjik", two, (mats[:, 0, 0], mats[:, 0, 1]))
    mixed = complex_einsum("srj,jik->srik", (mid[:, 0], mid[:, 1]), (whole[:, 0], whole[:, 1]))
    corr_re = jnp.sum(mixed[0] * one[0] - mixed[1] * one[1], axis=(1, 2, 3))
    corr_im = jnp.sum(mixed[0] * one[1] + mixed[1] * one[0], axis=(1, 2, 3))
    combos = spin_choice.shape[0]
    flat = jnp.stack([corr_re, corr_im], -1) * corr_scale
    tile = jnp.zeros((8, 128), jnp.float32).at[:combos, :2].set(flat)
    correlator = sum_space(tile, n)[:combos, :2]
    return (out[None], correlator[None])


def solution(mesh):
    placed = (P("tm", None, None, None, "space"), P("tm", None, None, None), P("tm"), P())
    return jax.shard_map(
        shards,
        mesh=mesh,
        in_specs=placed,
        out_specs=(P("tm", "space", None, None), P("tm", None, None)),
        check_vma=False,
    )
```

time: 347 us -> 131 us (0.38); the launches traced: 342 us -> 130 us
  waiting for transfers between devices: 106 us -> 0 us
  local copies, waits for them, and re-layouts: 97.5 us -> 29.2 us
  matrix products: 76.3 us -> 27.1 us
  Pallas kernels: 0 us -> 45.9 us
  blocking collectives: 15.2 us -> 0 us
  between operations: 14.7 us -> 1.6 us
  loops' own time: 12.9 us -> 0 us
  other arithmetic: 18.9 us -> 26.6 us
    psum x1 -> x0, waiting for transfers between devices: 67.9 us -> none  [shards(): lax.psum(elemental_rows(vec_re, vec_im, lead_re, lead_im, 0, nvec, factor...]
    dot_general x77 -> x12, matrix products: 76.3 us -> 27.1 us  [dot(): return jnp.einsum(form, a, b, precision=exact_mode)]
    pallas_call x0 -> x2, Pallas kernels: none -> 45.9 us  [the longest x1 38.3 us: elementals(): pl.pallas_call(functools.partial(elementals_kernel, n, times, scale), out...]
    all_gather x2 -> x0, waiting for transfers between devices: 38.1 us -> none  [the longest x1 25.2 us: shards(): every_time = lax.all_gather(own[None], 'tm', axis=0, tiled=True)]
    slice x39 -> x7, local copies, waits for them, and re-layouts: 32.9 us -> 5.42 us  [the longest x4 4.07 us: unpack(): low_left, mixed = (rows[..., :half], rows[..., half:])]
    psum x1 -> x0, blocking collectives: 15.2 us -> none  [shards(): correlator = lax.psum(partial_corr, 'space') * corr_factor]
    dynamic_slice x19 -> x2, local copies, waits for them, and re-layouts: 14.9 us -> 0.93 us  [the longest x1 0.92 us: shards(): lax.dynamic_index_in_dim(sinks, times - shift_steps[0] - 1, 0, keepdims=F...]
    another operation x40 -> x8, local copies, waits for them, and re-layouts: 17.9 us -> 4.4 us  [the longest x6 4.21 us: unpack(): rows = jnp.transpose(packed.reshape(half, count, 2, nvec), (1, 2, 0, 3))]
  transfers between devices with their start and end apart: 3 -> 0, of which waited for: 3 -> 0; matrix products, arithmetic and copies ran while one was open for 5% -> 0% of each run, Pallas kernels for 0% -> 0%
where the time goes in v1:
time: 131 us; the launch traced here: 130 us
  Pallas kernels  45.9 us (35%)
  local copies, waits for them, and re-layouts  29.2 us (22%)
  matrix products  27.1 us (21%)
  other arithmetic  26.6 us (20%)
  between operations  1.6 us (1%)
    pallas_call x1, Pallas kernels, elementals(): pl.pallas_call(functools.partial(elementals_kernel, n, times, scale), out...  38.3 us
    dot_general x12, matrix products, dot(): return jnp.einsum(form, a, b, precision=exact_mode)  27.1 us
    pallas_call x1, Pallas kernels, sum_space(): pl.pallas_call(functools.partial(sum_kernel, n), out_shape=jax.ShapeDtype...  7.62 us
    neg x3, other arithmetic, unpack(): return -jnp.concatenate([top, bottom], axis=-2)  7.48 us
    concatenate x2, local copies, waits for them, and re-layouts, unpack(): top = jnp.concatenate([upper - flip(upper), -flip(low_left)], axis=-1)  6.31 us
    select_n x3, local copies, waits for them, and re-layouts, unpack(): lower = jnp.tril(mixed, -1)  4.28 us
    sub x3, other arithmetic, unpack(): bottom = jnp.concatenate([low_left, lower - flip(lower)], axis=-1)  4.22 us
    another operation x6, local copies, waits for them, and re-layouts, unpack(): rows = jnp.transpose(packed.reshape(half, count, 2, nvec), (1, 2, 0, 3))  4.21 us

profile of v1, /device:TPU:0, one launch (start us, length us, event | category | flops | bytes accessed | tf_op | source)
XLA Modules:
  0.0 130.4 jit_solution(15703068839288683089)
XLA Ops:
  0.6 0.0 copy-start
  0.6 38.3 %elementals.1 = (f32[256,128]{1,0:T(8,128)}, f32[8,256,128]{2,1,0:T(8,128)}, f32[3,256,128]{2,1,0:T(8,128)}) custom-call(f32[2,3,64,256]{3,2,1,0:T(8,128)} %bitcast.157), custom_call_target="tpu_custom_call" | custom-call | tf_op jit(solution)/shard_map/elementals/pallas_call | solution.py:215
  38.9 1.1 reshape_reshape.9
  40.0 0.1 copy.122
  40.2 0.1 copy.39
  40.3 0.8 fusion.21
  41.0 0.1 copy.41
  41.2 0.8 copy.42
  42.7 0.9 constant_dynamic-slice_fusion
  43.6 0.2 reshape_reshape.11
  43.8 0.1 copy.121
  43.9 0.8 negate_bitcast_fusion.1
  44.7 0.1 copy.55
  44.9 0.1 copy.37
  45.0 0.1 broadcast_select_fusion.3
  45.1 0.0 copy-start.5
  45.1 0.1 copy.56
  45.2 0.1 copy.38
  45.4 0.8 bitcast_subtract_fusion.3
  46.2 0.0 copy-done.5
  46.2 1.2 maximum_negate_fusion.1
  47.4 0.2 copy.85
  47.6 1.0 reshape.83
  48.6 0.0 copy-done.4
  48.6 1.1 copy_bitcast_fusion.1
  49.7 2.5 %reshape_reshape.10 = f32[32,64,2,64]{3,2,1,0:T(2,128)S(1)} reshape(f32[32,8,8,128]{3,2,1,0:T(8,128)} %copy_bitcast_fusion.1) | data formatting | bytes 2097152 | tf_op jit(solution)/shard_map/reshape;reshape | solution.py:288
  52.2 0.3 copy.120
  52.5 3.1 %negate_bitcast_fusion = (f32[64,2,32,32]{2,0,3,1:T(8,128)}, f32[64,2,32,32]{3,0,2,1:T(8,128)}, f32[64,2,32,32]{3,0,2,1:T(8,128)S(1)}) fusion(f32[64,2,32,64]{3,0,2,1:T(8,128)S(1)} %bitcast.154), kind=kLoop, calls=%fused_computation.8 | loop fusion | flops 131072 | bytes 2621440 | tf_op jit(solution)/shard_map/neg | solution.py:293
  55.6 3.0 %copy.47 = f32[64,2,32,32]{2,0,3,1:T(8,128)} copy(f32[64,2,32,32]{3,0,2,1:T(8,128)S(1)} %get-tuple-element.28) | data formatting | bytes 1048576 | tf_op jit(solution)/shard_map/slice | solution.py:289
  58.6 3.5 %broadcast_select_fusion.1 = (f32[64,2,32,32]{2,0,3,1:T(8,128)S(1)}, f32[64,2,32,32]{2,0,3,1:T(8,128)}) fusion(f32[64,2,32,32]{2,0,3,1:T(8,128)} %copy.47, pred[32,32]{0,1:T(8,128)(4,1)S(1)} %iota_compare_fusion.1, pred[32,32]{0,1:T(8,128)(4,1)S(1)} %iota_compare_fusion), kind=kLoop, calls=%fused_computation.31 | loop fusion | flops 262144 | bytes 1574912 | tf_op jit(solution)/shard_map/jit(triu)/select_n | solution.py:290
  62.1 4.0 %copy.50 = f32[64,2,32,32]{3,0,2,1:T(8,128)} copy(f32[64,2,32,32]{2,0,3,1:T(8,128)} %get-tuple-element.25) | data formatting | bytes 1048576 | tf_op jit(solution)/shard_map/jit(tril)/select_n | solution.py:291
  66.1 4.1 %bitcast_subtract_fusion = f32[64,2,32,32]{3,0,2,1:T(8,128)} fusion(f32[64,2,32,32]{3,0,2,1:T(8,128)} %copy.50, f32[64,2,32,32]{2,0,3,1:T(8,128)} %get-tuple-element.25), kind=kLoop, calls=%fused_computation.5 | loop fusion | flops 131072 | bytes 1572864 | tf_op jit(solution)/shard_map/sub | solution.py:294
  70.3 3.0 %copy.48 = f32[64,2,32,32]{3,0,2,1:T(8,128)} copy(f32[64,2,32,32]{2,0,3,1:T(8,128)S(1)} %get-tuple-element.24) | data formatting | bytes 1048576 | tf_op jit(solution)/shard_map/jit(triu)/select_n | solution.py:290
  73.2 2.1 %bitcast_subtract_fusion.1 = f32[64,2,32,32]{2,0,3,1:T(8,128)S(1)} fusion(f32[64,2,32,32]{2,0,3,1:T(8,128)S(1)} %get-tuple-element.24, f32[64,2,32,32]{3,0,2,1:T(8,128)} %copy.48), kind=kLoop, calls=%fused_computation.6 | loop fusion | flops 131072 | bytes 1572864 | tf_op jit(solution)/shard_map/sub | solution.py:293
  75.4 0.1 copy-done.3
  75.5 2.5 %pad_maximum_fusion = f32[64,2,32,64]{2,0,3,1:T(8,128)} fusion(f32[64,2,32,32]{2,0,3,1:T(8,128)S(1)} %copy-done.3, f32[64,2,32,32]{2,0,3,1:T(8,128)S(1)} %bitcast_subtract_fusion.1), kind=kLoop, calls=%fused_computation.1 | loop fusion | flops 262144 | bytes 2097152 | tf_op jit(solution)/shard_map/concatenate | solution.py:293
  78.0 5.4 %copy.51 = f32[64,2,32,64]{3,0,2,1:T(8,128)} copy(f32[64,2,32,64]{2,0,3,1:T(8,128)} %pad_maximum_fusion) | data formatting | bytes 2097152 | tf_op jit(solution)/shard_map/concatenate | solution.py:293
  83.4 5.2 %maximum_negate_fusion = f32[64,2,64,64]{3,0,2,1:T(8,128)} fusion(f32[64,2,32,32]{3,0,2,1:T(8,128)} %bitcast_subtract_fusion, f32[64,2,32,32]{3,0,2,1:T(8,128)S(1)} %copy-done.2, f32[64,2,32,64]{3,0,2,1:T(8,128)} %copy.51), kind=kLoop, calls=%fused_computation.2 | loop fusion | flops 1572864 | bytes 4194304 | tf_op jit(solution)/shard_map/neg | solution.py:295
  88.5 0.1 reshape.64
  88.6 1.0 gather_fusion
  89.6 0.5 reshape.60
  90.1 2.7 %fusion.1 = f32[4,8,64,64]{3,1,2,0:T(8,128)S(1)} fusion(f32[64,2,64,64]{3,0,2,1:T(8,128)} %maximum_negate_fusion, f32[4,2,8,64]{3,2,0,1:T(8,128)S(1)} %copy_bitcast_fusion.4), kind=kOutput, calls=%fused_computation.10 | convolution fusion | flops 100663296 | bytes 2637824 | tf_op jit(solution)/shard_map/srj,jik->srik/dot_general | solution.py:300
  92.9 2.7 %fusion.4 = f32[4,8,64,64]{3,1,2,0:T(8,128)S(1)} fusion(f32[4,8,64,64]{3,1,2,0:T(8,128)S(1)} %fusion.1, f32[64,2,64,64]{3,0,2,1:T(8,128)} %maximum_negate_fusion, f32[4,2,8,64]{3,2,0,1:T(8,128)S(1)} %copy_bitcast_fusion.4), kind=kOutput, calls=%fused_computation.13 | convolution fusion | flops 100794368 | bytes 3686400 | tf_op jit(solution)/shard_map/srj,jik->srik/dot_general | solution.py:300
  95.6 0.1 copy.59
  95.7 1.1 pad_maximum_fusion.1
  96.8 0.9 copy.60
  97.7 1.1 maximum_negate_fusion.2
  98.8 1.0 fusion.13
  99.8 1.0 fusion.6
  100.9 3.1 %fusion.20 = f32[4,64,8,64]{3,1,2,0:T(8,128)S(1)} fusion(f32[4,8,64,64]{2,3,1,0:T(8,128)S(1)} %fusion.6, f32[4,3,2,64,64]{4,3,2,1,0:T(8,128)S(1)} %reshape.60), kind=kOutput, calls=%fused_computation.59 | convolution fusion | flops 100663296 | bytes 1703936 | tf_op jit(solution)/shard_map/sjmk,smi->sjik/dot_general | solution.py:300
  104.0 1.0 fusion.14
  105.1 1.0 fusion.7
  106.1 3.4 %fusion.18 = f32[4,64,8,64]{3,1,2,0:T(8,128)S(1)} fusion(f32[4,8,64,64]{2,3,1,0:T(8,128)S(1)} %fusion.7, f32[4,3,2,64,64]{4,3,2,1,0:T(8,128)S(1)} %reshape.60), kind=kOutput, calls=%fused_computation.57 | convolution fusion | flops 100663296 | bytes 1703936 | tf_op jit(solution)/shard_map/sjmk,smi->sjik/dot_general | solution.py:300
  109.5 3.1 %fusion.17 = f32[4,64,8,64]{3,1,2,0:T(8,128)S(1)} fusion(f32[4,8,64,64]{2,3,1,0:T(8,128)S(1)} %fusion.6, f32[4,3,2,64,64]{4,3,2,1,0:T(8,128)S(1)} %reshape.60), kind=kOutput, calls=%fused_computation.56 | convolution fusion | flops 100663296 | bytes 1703936 | tf_op jit(solution)/shard_map/sjmk,smi->sjik/dot_general | solution.py:300
  112.6 3.1 %fusion.19 = f32[4,64,8,64]{3,1,2,0:T(8,128)S(1)} fusion(f32[4,8,64,64]{2,3,1,0:T(8,128)S(1)} %fusion.7, f32[4,3,2,64,64]{4,3,2,1,0:T(8,128)S(1)} %reshape.60), kind=kOutput, calls=%fused_computation.58 | convolution fusion | flops 100663296 | bytes 1703936 | tf_op jit(solution)/shard_map/sjmk,smi->sjik/dot_general | solution.py:300
  115.8 1.1 fusion
  116.9 3.6 %fusion.9 = (f32[4]{0:T(128)S(1)}, f32[4]{0:T(128)S(1)}) fusion(f32[4,8,64,64]{3,1,2,0:T(8,128)S(1)} %fusion.4, f32[4,64,8,64]{3,1,2,0:T(8,128)S(1)} %fusion.20, f32[4,64,8,64]{3,1,2,0:T(8,128)S(1)} %fusion.18, f32[4,64,8,64]{3,1,2,0:T(8,128)S(1)} %fusion.17, f32[4,64,8,64]{3,1,2,0:T(8,128)S(1)} %fusion.19, f32[4,8,64,64]{3,1,2,0:T(8,128)S(1)} %fusion, ...), kind=kOutput, calls=%fused_computation.22 | convolution fusion | flops 102105080 | bytes 8405024 | tf_op jit(solution)/shard_map/srj,jik->srik/dot_general | solution.py:300
  120.5 0.1 copy.72
  120.6 0.1 copy.71
  120.7 0.1 maximum_multiply_fusion
  120.8 0.6 scatter.4.x_ref
  121.4 7.6 %sum_space.1 = f32[8,128]{1,0:T(8,128)} custom-call(f32[8,128]{1,0:T(8,128)} %scatter.4.x_ref), custom_call_target="tpu_custom_call" | custom-call | tf_op jit(solution)/shard_map/sum_space/pallas_call | solution.py:272
  129.0 0.7 slice.91
  129.7 0.7 copy.73
  (18 shorter events, 0.2 us)
Async XLA Ops:
  0.6 87.9 %copy-start = (f32[1,16,2,4096]{3,2,1,0:T(2,128)S(1)}, f32[1,16,2,4096]{3,2,1,0:T(2,128)}, u32[]{:S(2)}) copy-start(f32[1,16,2,4096]{3,2,1,0:T(2,128)} %param.7) | copy-start | bytes 1572868
  45.1 1.1 copy-start.5
  46.2 2.4 %copy-start.4 = (f32[8,256,128]{2,1,0:T(8,128)S(1)}, f32[8,256,128]{2,1,0:T(8,128)}, u32[]{:S(2)}) copy-start(f32[8,256,128]{2,1,0:T(8,128)} %get-tuple-element.18) | copy-start | bytes 3145732
  73.2 2.2 %copy-start.3 = (f32[64,2,32,32]{2,0,3,1:T(8,128)S(1)}, f32[64,2,32,32]{2,0,3,1:T(8,128)}, u32[]{:S(2)}) copy-start(f32[64,2,32,32]{2,0,3,1:T(8,128)} %get-tuple-element.26) | copy-start | bytes 1572868
  78.0 5.4 %copy-start.2 = (f32[64,2,32,32]{3,0,2,1:T(8,128)S(1)}, f32[64,2,32,32]{3,0,2,1:T(8,128)}, u32[]{:S(2)}) copy-start(f32[64,2,32,32]{3,0,2,1:T(8,128)} %get-tuple-element.27) | copy-start | bytes 1572868
  83.4 5.2 %copy-start.6 = (s32[4,3]{1,0:T(4,128)S(1)}, s32[4,3]{1,0:T(4,128)}, u32[]{:S(2)}) copy-start(s32[4,3]{1,0:T(4,128)} %param.9) | copy-start | bytes 148
  109.5 6.3 %copy-start.1 = (f32[64,2,64,64]{3,0,2,1:T(8,128)S(1)}, f32[64,2,64,64]{3,0,2,1:T(8,128)}, u32[]{:S(2)}) copy-start(f32[64,2,64,64]{3,0,2,1:T(8,128)} %maximum_negate_fusion) | copy-start | bytes 6291460

commit v2 on v1

--- a/solution.py
+++ b/solution.py
@@ -10,7 +10,6 @@
 
 MESH = pl.DeviceIdType.MESH
 VM = pl.BlockSpec(memory_space=pltpu.VMEM)
-exact_mode = lax.Precision.HIGHEST
 NT_DIMS = (((1,), (1,)), ((), ()))
 
 
@@ -24,10 +23,12 @@
 
 
 def elementals_kernel(
-    n, times, scale, v_ref, own_ref, full_ref, sink_ref,
-    lead, d_hi, d_lo, keep, give, pair_in, chip_in,
+    n, times, scale, corr_scale, v_ref, mats_ref, shift_ref, spin_ref, out_ref, corr_ref,
+    own_ref, full_ref, sink_ref, lead, d_hi, d_lo, keep, give, pair_in, chip_in,
+    right_hi, right_lo, half_hi, half_lo, weight, mixed_rows, chosen, tile_ref, box,
     pair_send, pair_recv, chip_send, chip_recv,
     own_send, own_recv, fwd_send, fwd_recv, tm_send, tm_recv,
+    sum_send, sum_recv,
 ):
     me = lax.axis_index("space")
     tm = lax.axis_index("tm")
@@ -43,16 +44,13 @@
     group = 16 // own
 
     barrier = pltpu.get_barrier_semaphore()
-    pl.semaphore_signal(barrier, inc=1, device_id=(tm, mate), device_id_type=MESH)
-    for r in range(1, chips):
-        pl.semaphore_signal(
-            barrier, inc=1, device_id=(tm, (chip + r) % chips * 2 + core), device_id_type=MESH
-        )
+    for r in range(1, n):
+        pl.semaphore_signal(barrier, inc=1, device_id=(tm, (me + r) % n), device_id_type=MESH)
     for r in range(1, times):
         pl.semaphore_signal(
             barrier, inc=1, device_id=((tm + r) % times, me), device_id_type=MESH
         )
-    pl.semaphore_wait(barrier, 1 + chips - 1 + times - 1)
+    pl.semaphore_wait(barrier, n - 1 + times - 1)
 
     for kind in range(2):
         for a in range(3):
@@ -184,156 +182,210 @@
             device_id=(tm, mate), device_id_type=MESH,
         )
 
+    for r in range(1, times):
+        tm_copy(r).start()
     for r in range(1, chips):
         own_copy(r).start()
-    for r in range(1, times):
-        tm_copy(r).start()
     own_copy(0).start()
     full_ref[me] = own_ref[...]
+
+    row = lax.broadcasted_iota(jnp.int32, (half, lanes), 0)
+    lane = lax.broadcasted_iota(jnp.int32, (half, lanes), 1)
+    spot = lane % nvec
+    left = spot < half
+    real = lane < nvec
+    minus_plus = jnp.where(lax.broadcasted_iota(jnp.int32, (nvec, lanes), 1) < nvec, -1.0, 1.0)
+
+    def dense(p):
+        t = jnp.transpose(jnp.concatenate([p] * (lanes // half), axis=0))
+        base = jnp.where(real, t[:half], t[nvec:nvec + half])
+        mixed = jnp.where(real, t[half:nvec], t[nvec + half:])
+        moved = pltpu.roll(p, lanes - half, 1)
+        zero = jnp.zeros_like(p)
+        upper = jnp.where(spot > row, moved, jnp.where(spot < row, -mixed, zero))
+        lower = jnp.where(spot - half < row, p, jnp.where(spot - half > row, -mixed, zero))
+        return jnp.where(left, upper, -base), jnp.where(left, p, lower)
+
+    for j in range(own):
+        top, bottom = dense(own_ref[pl.ds(j, half, stride=own), :])
+        matrix = -jnp.concatenate([top, bottom], axis=0)
+        out_ref[j, 0] = matrix[:, :nvec]
+        out_ref[j, 1] = pltpu.roll(matrix, nvec, 1)[:, :nvec]
+
+    combos = spin_ref.shape[0]
+    for s in range(combos):
+        for q in range(2):
+            spins = mats_ref[spin_ref[s, 2 * q]]
+            at = (s * 2 + q) * lanes
+            top_hi, top_lo = halves(spins)
+            low_hi, low_lo = halves(-minus_plus * pltpu.roll(spins, nvec, 1))
+            right_hi[0:nvec, at:at + lanes] = top_hi
+            right_lo[0:nvec, at:at + lanes] = top_lo
+            right_hi[nvec:lanes, at:at + lanes] = low_hi
+            right_lo[nvec:lanes, at:at + lanes] = low_lo
+
+    def dot3(a_hi, a_lo, b_hi, b_lo):
+        def dot(a, b):
+            return jnp.dot(a, b, preferred_element_type=jnp.float32)
+
+        return dot(a_hi, b_hi) + (dot(a_hi, b_lo) + dot(a_lo, b_hi))
+
+    for r in range(1, times):
+        tm_copy(r).wait_recv()
+    chosen[...] = sink_ref[jnp.clip(times - 1 - shift_ref[0], 0, times - 2)]
+    for j in range(own):
+        top, bottom = dense(chosen[pl.ds(j, half, stride=own), :])
+        hi, lo = halves(jnp.concatenate([top, bottom], axis=0))
+        got = dot3(hi, lo, right_hi[...], right_lo[...])
+        hi, lo = halves(got)
+        for s in range(combos):
+            for q in range(2):
+                at = (s * 2 + q) * lanes
+                where = (s, pl.ds(q * nvec, nvec), pl.ds(j * lanes, lanes))
+                half_hi[where] = hi[:, at:at + lanes]
+                half_lo[where] = lo[:, at:at + lanes]
     for r in range(1, chips):
         own_copy(r).wait_recv()
         forward(r).start()
+    for s in range(combos):
+        both = jnp.concatenate(
+            [mats_ref[spin_ref[s, 2]], mats_ref[spin_ref[s, 0]]], axis=0
+        )
+        hi, lo = halves(jnp.transpose(both))
+        got = dot3(hi, lo, half_hi[s], half_lo[s])
+        for j in range(own):
+            at = j * lanes
+            whole = got[:nvec, at:at + lanes] + minus_plus * pltpu.roll(
+                got[nvec:, at:at + lanes], nvec, 1
+            )
+            bent = jnp.where(
+                jnp.logical_or(left, spot - half < row),
+                whole[half:], pltpu.roll(whole[:half], half, 1),
+            )
+            weight[pl.ds((s * own + j) * half, half), :] = bent
+
+    mid = []
+    for s in range(combos):
+        which = spin_ref[s, 1]
+        if own % 8 == 0:
+            mid.append(mats_ref[which, pl.ds(pl.multiple_of(me * own, own), own), :])
+        else:
+            for r in range(own):
+                mid.append(mats_ref[which, pl.ds(me * own + r, 1), :])
+    mid = jnp.concatenate(mid, axis=0)
+    count = combos * own
+    mid = jnp.concatenate([mid[:, :nvec], pltpu.roll(mid, nvec, 1)[:, :nvec]], axis=0)
+    mid_hi, mid_lo = halves(mid)
+    own_copy(0).wait_recv()
+    for r in range(1, chips):
+        forward(r).wait_recv()
+    sign = jnp.where(lax.broadcasted_iota(jnp.int32, (count, lanes), 1) < nvec, -1.0, 1.0)
+    for k in range(half):
+        pieces = [full_ref[d, k * own:(k + 1) * own, :] for d in range(n)]
+        hi, lo = halves(jnp.concatenate(pieces, axis=0))
+        got = dot3(mid_hi, mid_lo, hi, lo)
+        mixed_rows[pl.ds(k * count, count), :] = got[:count] + sign * pltpu.roll(got[count:], nvec, 1)
+
+    straight, crossed = [], []
+    for s in range(combos):
+        one = jnp.zeros((half, lanes), jnp.float32)
+        two = jnp.zeros((half, lanes), jnp.float32)
+        for j in range(own):
+            at = s * own + j
+            value = mixed_rows[pl.ds(at, half, stride=count), :]
+            factor = weight[pl.ds(at * half, half), :]
+            one = one + value * factor
+            two = two + value * pltpu.roll(factor, nvec, 1)
+        straight.append(jnp.sum(jnp.where(real, one, -one), axis=0, keepdims=True))
+        crossed.append(jnp.sum(two, axis=0, keepdims=True))
+    tile_ref[...] = jnp.concatenate(straight + crossed, axis=0)
+
+    def sum_copy(r):
+        return pltpu.make_async_remote_copy(
+            tile_ref, box.at[r - 1], sum_send.at[r - 1], sum_recv.at[r - 1],
+            device_id=(tm, (me + r) % n), device_id_type=MESH,
+        )
+
+    for r in range(1, n):
+        sum_copy(r).start()
     for s in range(chips):
         pair_copy(s).wait_send()
     for s in range(chips - 1):
         chip_copy(s).wait_send()
     for r in range(1, times):
-        tm_copy(r).wait()
-    own_copy(0).wait()
+        tm_copy(r).wait_send()
+    own_copy(0).wait_send()
     for r in range(1, chips):
         own_copy(r).wait_send()
-        forward(r).wait()
-
-
-def elementals(vec, n, times, scale):
+        forward(r).wait_send()
+    answer = tile_ref[...]
+    for r in range(1, n):
+        sum_copy(r).wait_recv()
+        answer = answer + box[r - 1]
+    lines = jnp.sum(answer, axis=1, keepdims=True) * corr_scale
+    corr_ref[...] = jnp.concatenate([lines[:combos], lines[combos:]], axis=1)
+    for r in range(1, n):
+        sum_copy(r).wait_send()
+
+
+def shards(vectors, perambulators, shift_steps, spin_choice):
+    vec = vectors[0]
     _, _, nvec, sites = vec.shape
-    own, half = nvec // n, nvec // 2
+    spin_pairs = perambulators.shape[1]
+    combos = spin_choice.shape[0]
+    n = lax.axis_size("space")
+    times = lax.axis_size("tm")
+    own, half, lanes = nvec // n, nvec // 2, 2 * nvec
     chips = n // 2
-    tile = (half * own, 2 * nvec)
-    f32 = jnp.float32
+    scale = 1.0 / math.sqrt(24.0 * sites * n)
+    corr_scale = 0.25 / (nvec * math.sqrt(nvec))
+    mats = perambulators[0].reshape(spin_pairs, 2, nvec, nvec)
+    mats = jnp.transpose(mats, (0, 2, 1, 3)).reshape(spin_pairs, nvec, lanes)
+    tile = (half * own, lanes)
+    f32, bf16 = jnp.float32, jnp.bfloat16
     dma = pltpu.SemaphoreType.DMA
-    return pl.pallas_call(
-        functools.partial(elementals_kernel, n, times, scale),
+    smem = pl.BlockSpec(memory_space=pltpu.SMEM)
+    out, correlator = pl.pallas_call(
+        functools.partial(elementals_kernel, n, times, scale, corr_scale),
         out_shape=(
-            jax.ShapeDtypeStruct(tile, f32),
-            jax.ShapeDtypeStruct((n,) + tile, f32),
-            jax.ShapeDtypeStruct((times - 1,) + tile, f32),
+            jax.ShapeDtypeStruct((own, 2, nvec, nvec), f32),
+            jax.ShapeDtypeStruct((combos, 2), f32),
         ),
-        in_specs=[VM],
-        out_specs=(VM, VM, VM),
+        in_specs=[VM, VM, smem, smem],
+        out_specs=(VM, VM),
         scratch_shapes=[
-            pltpu.VMEM((2, 4 * nvec, 6 * sites), jnp.bfloat16),
-            pltpu.VMEM((2, half * own, 6 * sites), jnp.bfloat16),
-            pltpu.VMEM((2, half * own, 6 * sites), jnp.bfloat16),
+            pltpu.VMEM(tile, f32),
+            pltpu.VMEM((n,) + tile, f32),
+            pltpu.VMEM((times - 1,) + tile, f32),
+            pltpu.VMEM((2, 4 * nvec, 6 * sites), bf16),
+            pltpu.VMEM((2, half * own, 6 * sites), bf16),
+            pltpu.VMEM((2, half * own, 6 * sites), bf16),
             pltpu.VMEM((chips,) + tile, f32),
             pltpu.VMEM((chips,) + tile, f32),
             pltpu.VMEM((chips,) + tile, f32),
             pltpu.VMEM((chips - 1,) + tile, f32),
+            pltpu.VMEM((lanes, combos * 2 * lanes), bf16),
+            pltpu.VMEM((lanes, combos * 2 * lanes), bf16),
+            pltpu.VMEM((combos, 2 * nvec, own * lanes), bf16),
+            pltpu.VMEM((combos, 2 * nvec, own * lanes), bf16),
+            pltpu.VMEM((combos * own * half, lanes), f32),
+            pltpu.VMEM((combos * own * half, lanes), f32),
+            pltpu.VMEM(tile, f32),
+            pltpu.VMEM((2 * combos, lanes), f32),
+            pltpu.VMEM((n - 1, 2 * combos, lanes), f32),
             dma((chips,)), dma((chips,)),
             dma((chips - 1,)), dma((chips - 1,)),
             dma((chips,)), dma((chips,)),
             dma((chips - 1,)), dma((chips - 1,)),
             dma((times - 1,)), dma((times - 1,)),
+            dma((n - 1,)), dma((n - 1,)),
         ],
         compiler_params=pltpu.CompilerParams(
             collective_id=0, has_side_effects=True, vmem_limit_bytes=60 * 1024 * 1024
         ),
         name="elementals",
-    )(vec)
-
-
-def sum_kernel(n, x_ref, o_ref, box, send, recv):
-    me = lax.axis_index("space")
-    tm = lax.axis_index("tm")
-    barrier = pltpu.get_barrier_semaphore()
-    for r in range(1, n):
-        pl.semaphore_signal(barrier, inc=1, device_id=(tm, (me + r) % n), device_id_type=MESH)
-    pl.semaphore_wait(barrier, n - 1)
-
-    def copy(r):
-        return pltpu.make_async_remote_copy(
-            x_ref, box.at[r - 1], send.at[r - 1], recv.at[r - 1],
-            device_id=(tm, (me + r) % n), device_id_type=MESH,
-        )
-
-    for r in range(1, n):
-        copy(r).start()
-    total = x_ref[...]
-    for r in range(1, n):
-        copy(r).wait_recv()
-        total = total + box[r - 1]
-    o_ref[...] = total
-    for r in range(1, n):
-        copy(r).wait_send()
-
-
-def sum_space(x, n):
-    dma = pltpu.SemaphoreType.DMA
-    return pl.pallas_call(
-        functools.partial(sum_kernel, n),
-        out_shape=jax.ShapeDtypeStruct(x.shape, x.dtype),
-        in_specs=[VM],
-        out_specs=VM,
-        scratch_shapes=[
-            pltpu.VMEM((n - 1,) + x.shape, x.dtype), dma((n - 1,)), dma((n - 1,)),
-        ],
-        compiler_params=pltpu.CompilerParams(collective_id=1, has_side_effects=True),
-        name="sum_space",
-    )(x)
-
-
-def unpack(packed):
-    half, count, lanes = packed.shape
-    nvec = lanes // 2
-    rows = jnp.transpose(packed.reshape(half, count, 2, nvec), (1, 2, 0, 3))
-    low_left, mixed = rows[..., :half], rows[..., half:]
-    upper = jnp.triu(mixed, 1)
-    lower = jnp.tril(mixed, -1)
-    flip = lambda x: jnp.swapaxes(x, -1, -2)
-    top = jnp.concatenate([upper - flip(upper), -flip(low_left)], axis=-1)
-    bottom = jnp.concatenate([low_left, lower - flip(lower)], axis=-1)
-    return -jnp.concatenate([top, bottom], axis=-2)
-
-
-def complex_einsum(form, left, right):
-    def dot(a, b):
-        return jnp.einsum(form, a, b, precision=exact_mode)
-
-    return (
-        dot(left[0], right[0]) - dot(left[1], right[1]),
-        dot(left[0], right[1]) + dot(left[1], right[0]),
-    )
-
-
-def shards(vectors, perambulators, shift_steps, spin_choice):
-    vec = vectors[0]
-    nvec = vec.shape[2]
-    sites = vec.shape[3]
-    n = lax.axis_size("space")
-    times = lax.axis_size("tm")
-    own = nvec // n
-    scale = 1.0 / math.sqrt(24.0 * sites * n)
-    corr_scale = 0.25 / (nvec * math.sqrt(nvec))
-    mine, full, sinks = elementals(vec, n, times, scale)
-    packed = (nvec // 2, own, 2 * nvec)
-    out = unpack(mine.reshape(packed)).reshape(own, 2, nvec * nvec)
-    chosen = lax.dynamic_index_in_dim(sinks, times - shift_steps[0] - 1, 0, keepdims=False)
-    sink = unpack(chosen.reshape(packed))
-    full = jnp.transpose(full.reshape((n,) + packed), (1, 0, 2, 3))
-    whole = unpack(full.reshape(nvec // 2, nvec, 2 * nvec))
-    mats = perambulators[0][spin_choice].reshape(spin_choice.shape + (2, nvec, nvec))
-    first = lax.axis_index("space") * own
-    mid = lax.dynamic_slice_in_dim(mats[:, 1], first, own, 2)
-    two = complex_einsum("jml,slk->sjmk", (sink[:, 0], -sink[:, 1]), (mats[:, 2, 0], mats[:, 2, 1]))
-    one = complex_einsum("sjmk,smi->sjik", two, (mats[:, 0, 0], mats[:, 0, 1]))
-    mixed = complex_einsum("srj,jik->srik", (mid[:, 0], mid[:, 1]), (whole[:, 0], whole[:, 1]))
-    corr_re = jnp.sum(mixed[0] * one[0] - mixed[1] * one[1], axis=(1, 2, 3))
-    corr_im = jnp.sum(mixed[0] * one[1] + mixed[1] * one[0], axis=(1, 2, 3))
-    combos = spin_choice.shape[0]
-    flat = jnp.stack([corr_re, corr_im], -1) * corr_scale
-    tile = jnp.zeros((8, 128), jnp.float32).at[:combos, :2].set(flat)
-    correlator = sum_space(tile, n)[:combos, :2]
-    return (out[None], correlator[None])
+    )(vec, mats, shift_steps, spin_choice)
+    return (out.reshape(1, own, 2, nvec * nvec), correlator[None])
 
 
 def solution(mesh):

time: 131 us -> 52.8 us (0.40)
  matrix products: 27.1 us -> 0 us
  other arithmetic: 26.6 us -> 0 us
  local copies, waits for them, and re-layouts: 29.2 us -> 6.52 us
    dot_general x12 -> x0, matrix products: 27.1 us -> none  [dot(): return jnp.einsum(form, a, b, precision=exact_mode)]
    neg x5 -> x0, other arithmetic: 11.4 us -> none  [the longest x3 7.48 us: unpack(): return -jnp.concatenate([top, bottom], axis=-2)]
    select_n x6 -> x0, local copies, waits for them, and re-layouts: 7.52 us -> none  [the longest x3 4.28 us: unpack(): lower = jnp.tril(mixed, -1)]
    sub x5 -> x0, other arithmetic: 7.13 us -> none  [the longest x3 4.22 us: unpack(): bottom = jnp.concatenate([low_left, lower - flip(lower)], axis=-1)]
    concatenate x2 -> x0, local copies, waits for them, and re-layouts: 6.31 us -> none  [unpack(): top = jnp.concatenate([upper - flip(upper), -flip(low_left)], axis=-1)]
    slice x7 -> x0, local copies, waits for them, and re-layouts: 5.42 us -> none  [the longest x4 4.07 us: unpack(): low_left, mixed = (rows[..., :half], rows[..., half:])]
    select_n x3 -> x0, other arithmetic: 3.62 us -> none  [the longest x2 3.62 us: unpack(): upper = jnp.triu(mixed, 1)]
    concatenate x2 -> x0, other arithmetic: 3.57 us -> none  [unpack(): top = jnp.concatenate([upper - flip(upper), -flip(low_left)], axis=-1)]
where the time goes in v2:
time: 52.8 us; the launch traced here: 52.6 us
  Pallas kernels  44.8 us (85%)
  local copies, waits for them, and re-layouts  6.52 us (12%)
  between operations  1.31 us (2%)
    pallas_call x1, Pallas kernels, shards(): pl.pallas_call(functools.partial(elementals_kernel, n, times, scale, corr...  44.8 us
    another operation x2, local copies, waits for them, and re-layouts, shards(): mats = perambulators[0].reshape(spin_pairs, 2, nvec, nvec)  2.48 us
    reshape x1, local copies, waits for them, and re-layouts, shards(): return (out.reshape(1, own, 2, nvec * nvec), correlator[None])  2.01 us
    reshape x1, local copies, waits for them, and re-layouts, shards(): mats = jnp.transpose(mats, (0, 2, 1, 3)).reshape(spin_pairs, nvec, lanes)  1.38 us

profile of v2, /device:TPU:0, one launch (start us, length us, event | category | flops | bytes accessed | tf_op | source)
XLA Modules:
  0.0 52.6 jit_solution(7289513578410868226)
XLA Ops:
  0.6 1.7 %reshape_squeeze.3 = f32[16,2,64,64]{3,2,1,0:T(8,128)S(1)} reshape(f32[1,16,2,4096]{3,2,1,0:T(2,128)} %param.5) | data formatting | bytes 1048576 | tf_op jit(solution)/shard_map/reshape;squeeze | solution.py:342
  2.3 0.8 %copy.9 = f32[16,2,64,64]{3,1,2,0:T(2,128)S(1)} copy(f32[16,2,64,64]{3,2,1,0:T(8,128)S(1)} %reshape_squeeze.3) | data formatting | bytes 1048576 | tf_op jit(solution)/shard_map/reshape;squeeze | solution.py:342
  3.1 1.4 %reshape.10.mats_ref = f32[16,64,128]{2,1,0:T(8,128)} reshape(f32[16,64,2,64]{3,2,1,0:T(2,128)S(1)} %bitcast.7) | data formatting | bytes 1048576 | tf_op jit(solution)/shard_map/reshape | solution.py:343
  5.1 44.8 %elementals.1 = (f32[8,2,64,64]{3,2,1,0:T(8,128)}, f32[4,2]{1,0:T(4,128)}) custom-call(f32[2,3,64,256]{3,2,1,0:T(8,128)} %bitcast.8, f32[16,64,128]{2,1,0:T(8,128)} %reshape.10.mats_ref, s32[1]{0:T(128)S(6)} %copy.10.shift_ref, s32[4,3]{1,0:T(4,128)} %spin_ref.1), custom_call_target="tpu_custom_call" | custom-call | tf_op jit(solution)/shard_map/elementals/pallas_call | solution.py:348
  49.9 0.0 copy-start
  49.9 2.0 %reshape.11 = f32[1,8,2,4096]{3,2,1,0:T(2,128)} reshape(f32[8,2,64,64]{3,2,1,0:T(8,128)} %get-tuple-element.4) | data formatting | bytes 524288 | tf_op jit(solution)/shard_map/reshape | solution.py:388
  51.9 0.0 copy-done
  51.9 0.6 %copy.7 = f32[4,2]{0,1:T(2,128)} copy(f32[4,2]{1,0:T(4,128)S(1)} %copy-done) | data formatting | bytes 64 | tf_op jit(solution)/shard_map/elementals/pallas_call | solution.py:348
Async XLA Ops:
  49.9 2.0 %copy-start = (f32[4,2]{1,0:T(4,128)S(1)}, f32[4,2]{1,0:T(4,128)}, u32[]{:S(2)}) copy-start(f32[4,2]{1,0:T(4,128)} %get-tuple-element.5) | copy-start | bytes 100

commit v3 on v2

--- a/solution.py
+++ b/solution.py
@@ -25,7 +25,7 @@
 def elementals_kernel(
     n, times, scale, corr_scale, v_ref, mats_ref, shift_ref, spin_ref, out_ref, corr_ref,
     own_ref, full_ref, sink_ref, lead, d_hi, d_lo, keep, give, pair_in, chip_in,
-    right_hi, right_lo, half_hi, half_lo, weight, mixed_rows, chosen, tile_ref, box,
+    right_hi, right_lo, half_hi, half_lo, weight, mixed_rows, chosen, board, spin_mats, tile_ref, box,
     pair_send, pair_recv, chip_send, chip_recv,
     own_send, own_recv, fwd_send, fwd_recv, tm_send, tm_recv,
     sum_send, sum_recv,
@@ -206,16 +206,32 @@
         lower = jnp.where(spot - half < row, p, jnp.where(spot - half > row, -mixed, zero))
         return jnp.where(left, upper, -base), jnp.where(left, p, lower)
 
+    def weave(ref):
+        even = ref[pl.ds(0, half, stride=2), :]
+        odd = ref[pl.ds(1, half, stride=2), :]
+        return (
+            jnp.where(real, even, pltpu.roll(odd, nvec, 1)),
+            jnp.where(real, pltpu.roll(even, nvec, 1), odd),
+        )
+
     for j in range(own):
         top, bottom = dense(own_ref[pl.ds(j, half, stride=own), :])
-        matrix = -jnp.concatenate([top, bottom], axis=0)
-        out_ref[j, 0] = matrix[:, :nvec]
-        out_ref[j, 1] = pltpu.roll(matrix, nvec, 1)[:, :nvec]
+        board[0:half, :] = -top
+        board[half:nvec, :] = -bottom
+        even, odd = weave(board)
+        out_ref[j, pl.ds(0, half, stride=2), :] = even
+        out_ref[j, pl.ds(1, half, stride=2), :] = odd
 
     combos = spin_ref.shape[0]
     for s in range(combos):
+        for q in range(3):
+            board[...] = mats_ref[spin_ref[s, q]]
+            even, odd = weave(board)
+            spin_mats[s, q, pl.ds(0, half, stride=2), :] = even
+            spin_mats[s, q, pl.ds(1, half, stride=2), :] = odd
+    for s in range(combos):
         for q in range(2):
-            spins = mats_ref[spin_ref[s, 2 * q]]
+            spins = spin_mats[s, 2 * q]
             at = (s * 2 + q) * lanes
             top_hi, top_lo = halves(spins)
             low_hi, low_lo = halves(-minus_plus * pltpu.roll(spins, nvec, 1))
@@ -249,7 +265,7 @@
         forward(r).start()
     for s in range(combos):
         both = jnp.concatenate(
-            [mats_ref[spin_ref[s, 2]], mats_ref[spin_ref[s, 0]]], axis=0
+            [spin_mats[s, 2], spin_mats[s, 0]], axis=0
         )
         hi, lo = halves(jnp.transpose(both))
         got = dot3(hi, lo, half_hi[s], half_lo[s])
@@ -266,12 +282,11 @@
 
     mid = []
     for s in range(combos):
-        which = spin_ref[s, 1]
         if own % 8 == 0:
-            mid.append(mats_ref[which, pl.ds(pl.multiple_of(me * own, own), own), :])
+            mid.append(spin_mats[s, 1, pl.ds(pl.multiple_of(me * own, own), own), :])
         else:
             for r in range(own):
-                mid.append(mats_ref[which, pl.ds(me * own + r, 1), :])
+                mid.append(spin_mats[s, 1, pl.ds(me * own + r, 1), :])
     mid = jnp.concatenate(mid, axis=0)
     count = combos * own
     mid = jnp.concatenate([mid[:, :nvec], pltpu.roll(mid, nvec, 1)[:, :nvec]], axis=0)
@@ -339,7 +354,7 @@
     chips = n // 2
     scale = 1.0 / math.sqrt(24.0 * sites * n)
     corr_scale = 0.25 / (nvec * math.sqrt(nvec))
-    mats = perambulators[0].reshape(spin_pairs, 2, nvec, nvec)
+    mats = perambulators[0].reshape(spin_pairs, 2, half, lanes)
     mats = jnp.transpose(mats, (0, 2, 1, 3)).reshape(spin_pairs, nvec, lanes)
     tile = (half * own, lanes)
     f32, bf16 = jnp.float32, jnp.bfloat16
@@ -348,7 +363,7 @@
     out, correlator = pl.pallas_call(
         functools.partial(elementals_kernel, n, times, scale, corr_scale),
         out_shape=(
-            jax.ShapeDtypeStruct((own, 2, nvec, nvec), f32),
+            jax.ShapeDtypeStruct((own, nvec, lanes), f32),
             jax.ShapeDtypeStruct((combos, 2), f32),
         ),
         in_specs=[VM, VM, smem, smem],
@@ -371,6 +386,8 @@
             pltpu.VMEM((combos * own * half, lanes), f32),
             pltpu.VMEM((combos * own * half, lanes), f32),
             pltpu.VMEM(tile, f32),
+            pltpu.VMEM((nvec, lanes), f32),
+            pltpu.VMEM((combos, 3, nvec, lanes), f32),
             pltpu.VMEM((2 * combos, lanes), f32),
             pltpu.VMEM((n - 1, 2 * combos, lanes), f32),
             dma((chips,)), dma((chips,)),
@@ -385,6 +402,7 @@
         ),
         name="elementals",
     )(vec, mats, shift_steps, spin_choice)
+    out = jnp.transpose(out.reshape(own, half, 2, lanes), (0, 2, 1, 3))
     return (out.reshape(1, own, 2, nvec * nvec), correlator[None])
 
 

time: 52.8 us -> 49.1 us (0.930)
  local copies, waits for them, and re-layouts: 6.52 us -> 2.99 us
    reshape x2 -> x0, local copies, waits for them, and re-layouts: 3.39 us -> none  [the longest x1 2.01 us: shards(): return (out.reshape(1, own, 2, nvec * nvec), correlator[None])]
    another operation x2 -> x0, local copies, waits for them, and re-layouts: 2.48 us -> none  [shards(): mats = perambulators[0].reshape(spin_pairs, 2, nvec, nvec)]
    unnamed x2 -> x3, local copies, waits for them, and re-layouts: 0.01 us -> 2.35 us
where the time goes in v3:
time: 49.1 us; the launch traced here: 48.9 us
  Pallas kernels  44.6 us (91%)
  local copies, waits for them, and re-layouts  2.99 us (6%)
  between operations  1.29 us (3%)
    pallas_call x1, Pallas kernels, shards(): pl.pallas_call(functools.partial(elementals_kernel, n, times, scale, corr...  44.6 us
    unnamed x3, local copies, waits for them, and re-layouts  2.35 us

profile of v3, /device:TPU:0, one launch (start us, length us, event | category | flops | bytes accessed | tf_op | source)
XLA Modules:
  0.0 48.9 jit_solution(14009356305820512474)
XLA Ops:
  1.3 44.6 %elementals.1 = (f32[8,64,128]{2,1,0:T(8,128)}, f32[4,2]{1,0:T(4,128)}) custom-call(f32[2,3,64,256]{3,2,1,0:T(8,128)} %bitcast.13, f32[16,64,128]{2,1,0:T(8,128)} %bitcast.12, s32[1]{0:T(128)S(6)} %copy.10.shift_ref, s32[4,3]{1,0:T(4,128)} %spin_ref.1), custom_call_target="tpu_custom_call" | custom-call | tf_op jit(solution)/shard_map/elementals/pallas_call | solution.py:363
  45.9 0.0 copy-start
  45.9 0.7 %copy-done = f32[4,2]{1,0:T(4,128)S(1)} copy-done((f32[4,2]{1,0:T(4,128)S(1)}, f32[4,2]{1,0:T(4,128)}, u32[]{:S(2)}) %copy-start) | copy-done | bytes 56
  46.6 0.6 %copy.8 = f32[4,2]{0,1:T(2,128)} copy(f32[4,2]{1,0:T(4,128)S(1)} %copy-done) | data formatting | bytes 64 | tf_op jit(solution)/shard_map/elementals/pallas_call | solution.py:363
  47.2 1.7 %copy.11 = f32[1,8,2,4096]{3,2,1,0:T(2,128)} copy(f32[1,8,2,4096]{3,2,1,0:T(2,128)} %bitcast.14) | data formatting | bytes 524288
Async XLA Ops:
  45.9 0.7 %copy-start = (f32[4,2]{1,0:T(4,128)S(1)}, f32[4,2]{1,0:T(4,128)}, u32[]{:S(2)}) copy-start(f32[4,2]{1,0:T(4,128)} %get-tuple-element.5) | copy-start | bytes 100

commit v4 on v3

--- a/solution.py
+++ b/solution.py
@@ -50,7 +50,6 @@
         pl.semaphore_signal(
             barrier, inc=1, device_id=((tm + r) % times, me), device_id_type=MESH
         )
-    pl.semaphore_wait(barrier, n - 1 + times - 1)
 
     for kind in range(2):
         for a in range(3):
@@ -141,54 +140,25 @@
             device_id=(tm, (chip + 1 + s) % chips * 2 + core), device_id_type=MESH,
         )
 
+    def give_block(s):
+        block((chip + 1 + s) % chips * 2 + 1 - core, give.at[s])
+
     def one_chip(s, carry):
-        z = (chip + 1 + s) % chips
-        block(z * 2 + 1 - core, give.at[s])
         pair_copy(s).start()
-        block(z * 2 + core, keep.at[s])
+        block((chip + 1 + s) % chips * 2 + core, keep.at[s])
         pair_copy(s).wait_recv()
         keep[s] = keep[s] + pair_in[s]
 
         @pl.when(s < chips - 1)
         def _():
             chip_copy(s).start()
+            give_block(s + 1)
 
         return carry
 
+    give_block(0)
+    pl.semaphore_wait(barrier, n - 1 + times - 1)
     lax.fori_loop(0, chips, one_chip, 0)
-    total = keep[chips - 1]
-    for s in range(chips - 1):
-        chip_copy(s).wait_recv()
-        total = total + chip_in[s]
-    own_ref[...] = total * scale
-
-    def tm_copy(r):
-        return pltpu.make_async_remote_copy(
-            own_ref, sink_ref.at[r - 1], tm_send.at[r - 1], tm_recv.at[r - 1],
-            device_id=((tm + r) % times, me), device_id_type=MESH,
-        )
-
-    def own_copy(r):
-        target = mate if r == 0 else (chip + r) % chips * 2 + core
-        return pltpu.make_async_remote_copy(
-            own_ref, full_ref.at[me], own_send.at[r], own_recv.at[r],
-            device_id=(tm, target), device_id_type=MESH,
-        )
-
-    def forward(r):
-        slot = (chip + chips - r) % chips * 2 + core
-        return pltpu.make_async_remote_copy(
-            full_ref.at[slot], full_ref.at[slot], fwd_send.at[r - 1], fwd_recv.at[r - 1],
-            device_id=(tm, mate), device_id_type=MESH,
-        )
-
-    for r in range(1, times):
-        tm_copy(r).start()
-    for r in range(1, chips):
-        own_copy(r).start()
-    own_copy(0).start()
-    full_ref[me] = own_ref[...]
-
     row = lax.broadcasted_iota(jnp.int32, (half, lanes), 0)
     lane = lax.broadcasted_iota(jnp.int32, (half, lanes), 1)
     spot = lane % nvec
@@ -196,16 +166,6 @@
     real = lane < nvec
     minus_plus = jnp.where(lax.broadcasted_iota(jnp.int32, (nvec, lanes), 1) < nvec, -1.0, 1.0)
 
-    def dense(p):
-        t = jnp.transpose(jnp.concatenate([p] * (lanes // half), axis=0))
-        base = jnp.where(real, t[:half], t[nvec:nvec + half])
-        mixed = jnp.where(real, t[half:nvec], t[nvec + half:])
-        moved = pltpu.roll(p, lanes - half, 1)
-        zero = jnp.zeros_like(p)
-        upper = jnp.where(spot > row, moved, jnp.where(spot < row, -mixed, zero))
-        lower = jnp.where(spot - half < row, p, jnp.where(spot - half > row, -mixed, zero))
-        return jnp.where(left, upper, -base), jnp.where(left, p, lower)
-
     def weave(ref):
         even = ref[pl.ds(0, half, stride=2), :]
         odd = ref[pl.ds(1, half, stride=2), :]
@@ -213,14 +173,6 @@
             jnp.where(real, even, pltpu.roll(odd, nvec, 1)),
             jnp.where(real, pltpu.roll(even, nvec, 1), odd),
         )
-
-    for j in range(own):
-        top, bottom = dense(own_ref[pl.ds(j, half, stride=own), :])
-        board[0:half, :] = -top
-        board[half:nvec, :] = -bottom
-        even, odd = weave(board)
-        out_ref[j, pl.ds(0, half, stride=2), :] = even
-        out_ref[j, pl.ds(1, half, stride=2), :] = odd
 
     combos = spin_ref.shape[0]
     for s in range(combos):
@@ -239,6 +191,57 @@
             right_lo[0:nvec, at:at + lanes] = top_lo
             right_hi[nvec:lanes, at:at + lanes] = low_hi
             right_lo[nvec:lanes, at:at + lanes] = low_lo
+
+    total = keep[chips - 1]
+    for s in range(chips - 1):
+        chip_copy(s).wait_recv()
+        total = total + chip_in[s]
+    own_ref[...] = total * scale
+
+    def tm_copy(r):
+        return pltpu.make_async_remote_copy(
+            own_ref, sink_ref.at[r - 1], tm_send.at[r - 1], tm_recv.at[r - 1],
+            device_id=((tm + r) % times, me), device_id_type=MESH,
+        )
+
+    def own_copy(r):
+        target = mate if r == 0 else (chip + r) % chips * 2 + core
+        return pltpu.make_async_remote_copy(
+            own_ref, full_ref.at[me], own_send.at[r], own_recv.at[r],
+            device_id=(tm, target), device_id_type=MESH,
+        )
+
+    def forward(r):
+        slot = (chip + chips - r) % chips * 2 + core
+        return pltpu.make_async_remote_copy(
+            full_ref.at[slot], full_ref.at[slot], fwd_send.at[r - 1], fwd_recv.at[r - 1],
+            device_id=(tm, mate), device_id_type=MESH,
+        )
+
+    for r in range(1, times):
+        tm_copy(r).start()
+    for r in range(1, chips):
+        own_copy(r).start()
+    own_copy(0).start()
+    full_ref[me] = own_ref[...]
+
+    def dense(p):
+        t = jnp.transpose(jnp.concatenate([p] * (lanes // half), axis=0))
+        base = jnp.where(real, t[:half], t[nvec:nvec + half])
+        mixed = jnp.where(real, t[half:nvec], t[nvec + half:])
+        moved = pltpu.roll(p, lanes - half, 1)
+        zero = jnp.zeros_like(p)
+        upper = jnp.where(spot > row, moved, jnp.where(spot < row, -mixed, zero))
+        lower = jnp.where(spot - half < row, p, jnp.where(spot - half > row, -mixed, zero))
+        return jnp.where(left, upper, -base), jnp.where(left, p, lower)
+
+    for j in range(own):
+        top, bottom = dense(own_ref[pl.ds(j, half, stride=own), :])
+        board[0:half, :] = -top
+        board[half:nvec, :] = -bottom
+        even, odd = weave(board)
+        out_ref[j, pl.ds(0, half, stride=2), :] = even
+        out_ref[j, pl.ds(1, half, stride=2), :] = odd
 
     def dot3(a_hi, a_lo, b_hi, b_lo):
         def dot(a, b):

time: 49.1 us -> 47.1 us (0.959)
  Pallas kernels: 44.6 us -> 42.6 us
    pallas_call x1, Pallas kernels: 44.6 us -> 42.6 us  [shards(): pl.pallas_call(functools.partial(elementals_kernel, n, times, scale, corr...]
where the time goes in v4:
time: 47.1 us; the launch traced here: 46.9 us
  Pallas kernels  42.6 us (90%)
  local copies, waits for them, and re-layouts  2.99 us (6%)
  between operations  1.29 us (3%)
    pallas_call x1, Pallas kernels, shards(): pl.pallas_call(functools.partial(elementals_kernel, n, times, scale, corr...  42.6 us
    unnamed x3, local copies, waits for them, and re-layouts  2.35 us

profile of v4, /device:TPU:0, one launch (start us, length us, event | category | flops | bytes accessed | tf_op | source)
XLA Modules:
  0.0 46.9 jit_solution(12404553187884903741)
XLA Ops:
  1.3 42.6 %elementals.1 = (f32[8,64,128]{2,1,0:T(8,128)}, f32[4,2]{1,0:T(4,128)}) custom-call(f32[2,3,64,256]{3,2,1,0:T(8,128)} %bitcast.13, f32[16,64,128]{2,1,0:T(8,128)} %bitcast.12, s32[1]{0:T(128)S(6)} %copy.10.shift_ref, s32[4,3]{1,0:T(4,128)} %spin_ref.1), custom_call_target="tpu_custom_call" | custom-call | tf_op jit(solution)/shard_map/elementals/pallas_call | solution.py:366
  43.9 0.0 copy-start
  43.9 0.7 %copy-done = f32[4,2]{1,0:T(4,128)S(1)} copy-done((f32[4,2]{1,0:T(4,128)S(1)}, f32[4,2]{1,0:T(4,128)}, u32[]{:S(2)}) %copy-start) | copy-done | bytes 56
  44.5 0.6 %copy.8 = f32[4,2]{0,1:T(2,128)} copy(f32[4,2]{1,0:T(4,128)S(1)} %copy-done) | data formatting | bytes 64 | tf_op jit(solution)/shard_map/elementals/pallas_call | solution.py:366
  45.2 1.7 %copy.11 = f32[1,8,2,4096]{3,2,1,0:T(2,128)} copy(f32[1,8,2,4096]{3,2,1,0:T(2,128)} %bitcast.14) | data formatting | bytes 524288
Async XLA Ops:
  43.9 0.7 %copy-start = (f32[4,2]{1,0:T(4,128)S(1)}, f32[4,2]{1,0:T(4,128)}, u32[]{:S(2)}) copy-start(f32[4,2]{1,0:T(4,128)} %get-tuple-element.5) | copy-start | bytes 100

commit v5 on v4

--- a/solution.py
+++ b/solution.py
@@ -27,7 +27,7 @@
     own_ref, full_ref, sink_ref, lead, d_hi, d_lo, keep, give, pair_in, chip_in,
     right_hi, right_lo, half_hi, half_lo, weight, mixed_rows, chosen, board, spin_mats, tile_ref, box,
     pair_send, pair_recv, chip_send, chip_recv,
-    own_send, own_recv, fwd_send, fwd_recv, tm_send, tm_recv,
+    own_send, own_recv, line_send, line_recv, fwd_send, fwd_recv, tm_send, tm_recv,
     sum_send, sum_recv,
 ):
     me = lax.axis_index("space")
@@ -204,26 +204,57 @@
             device_id=((tm + r) % times, me), device_id_type=MESH,
         )
 
-    def own_copy(r):
-        target = mate if r == 0 else (chip + r) % chips * 2 + core
-        return pltpu.make_async_remote_copy(
-            own_ref, full_ref.at[me], own_send.at[r], own_recv.at[r],
-            device_id=(tm, target), device_id_type=MESH,
-        )
-
-    def forward(r):
-        slot = (chip + chips - r) % chips * 2 + core
-        return pltpu.make_async_remote_copy(
-            full_ref.at[slot], full_ref.at[slot], fwd_send.at[r - 1], fwd_recv.at[r - 1],
+    mate_copy = pltpu.make_async_remote_copy(
+        own_ref, full_ref.at[me], own_send.at[0], own_recv.at[0],
+        device_id=(tm, mate), device_id_type=MESH,
+    )
+
+    def slot_of(z):
+        return (z + chips) % chips * 2 + core
+
+    def hop(way, t):
+        held = slot_of(chip - way * (t - 1))
+        side = (1 - way) // 2
+        return pltpu.make_async_remote_copy(
+            full_ref.at[held], full_ref.at[held],
+            line_send.at[side, t - 1], line_recv.at[side, t - 1],
+            device_id=(tm, slot_of(chip + way)), device_id_type=MESH,
+        )
+
+    def to_mate(way, t):
+        held = slot_of(chip - way * t)
+        side = (1 - way) // 2
+        return pltpu.make_async_remote_copy(
+            full_ref.at[held], full_ref.at[held],
+            fwd_send.at[side, t - 1], fwd_recv.at[side, t - 1],
             device_id=(tm, mate), device_id_type=MESH,
         )
 
+    def has(z):
+        return jnp.logical_and(z >= 0, z < chips)
+
+    def sends(way, t):
+        return jnp.logical_and(has(chip + way), has(chip - way * (t - 1)))
+
+    def each_send(t, act):
+        for way in (1, -1):
+            pl.when(sends(way, t))(functools.partial(act, way, t))
+
+    def each_arrival(t, act):
+        for way in (1, -1):
+            pl.when(has(chip - way * t))(functools.partial(act, way, t))
+
+    def pass_on(t):
+        each_arrival(t, lambda way, t: hop(way, t).wait_recv())
+        if t + 1 < chips:
+            each_send(t + 1, lambda way, t: hop(way, t).start())
+        each_arrival(t, lambda way, t: to_mate(way, t).start())
+
+    full_ref[me] = own_ref[...]
+    each_send(1, lambda way, t: hop(way, t).start())
     for r in range(1, times):
         tm_copy(r).start()
-    for r in range(1, chips):
-        own_copy(r).start()
-    own_copy(0).start()
-    full_ref[me] = own_ref[...]
+    mate_copy.start()
 
     def dense(p):
         t = jnp.transpose(jnp.concatenate([p] * (lanes // half), axis=0))
@@ -242,6 +273,8 @@
         even, odd = weave(board)
         out_ref[j, pl.ds(0, half, stride=2), :] = even
         out_ref[j, pl.ds(1, half, stride=2), :] = odd
+
+    pass_on(1)
 
     def dot3(a_hi, a_lo, b_hi, b_lo):
         def dot(a, b):
@@ -263,9 +296,10 @@
                 where = (s, pl.ds(q * nvec, nvec), pl.ds(j * lanes, lanes))
                 half_hi[where] = hi[:, at:at + lanes]
                 half_lo[where] = lo[:, at:at + lanes]
-    for r in range(1, chips):
-        own_copy(r).wait_recv()
-        forward(r).start()
+        if j == own // 2 - 1:
+            pass_on(2)
+    for t in range(3, chips):
+        pass_on(t)
     for s in range(combos):
         both = jnp.concatenate(
             [spin_mats[s, 2], spin_mats[s, 0]], axis=0
@@ -294,9 +328,9 @@
     count = combos * own
     mid = jnp.concatenate([mid[:, :nvec], pltpu.roll(mid, nvec, 1)[:, :nvec]], axis=0)
     mid_hi, mid_lo = halves(mid)
-    own_copy(0).wait_recv()
-    for r in range(1, chips):
-        forward(r).wait_recv()
+    mate_copy.wait_recv()
+    for t in range(1, chips):
+        each_arrival(t, lambda way, t: to_mate(way, t).wait_recv())
     sign = jnp.where(lax.broadcasted_iota(jnp.int32, (count, lanes), 1) < nvec, -1.0, 1.0)
     for k in range(half):
         pieces = [full_ref[d, k * own:(k + 1) * own, :] for d in range(n)]
@@ -332,10 +366,10 @@
         chip_copy(s).wait_send()
     for r in range(1, times):
         tm_copy(r).wait_send()
-    own_copy(0).wait_send()
-    for r in range(1, chips):
-        own_copy(r).wait_send()
-        forward(r).wait_send()
+    mate_copy.wait_send()
+    for t in range(1, chips):
+        each_send(t, lambda way, t: hop(way, t).wait_send())
+        each_arrival(t, lambda way, t: to_mate(way, t).wait_send())
     answer = tile_ref[...]
     for r in range(1, n):
         sum_copy(r).wait_recv()
@@ -395,8 +429,9 @@
             pltpu.VMEM((n - 1, 2 * combos, lanes), f32),
             dma((chips,)), dma((chips,)),
             dma((chips - 1,)), dma((chips - 1,)),
-            dma((chips,)), dma((chips,)),
-            dma((chips - 1,)), dma((chips - 1,)),
+            dma((1,)), dma((1,)),
+            dma((2, chips - 1)), dma((2, chips - 1)),
+            dma((2, chips - 1)), dma((2, chips - 1)),
             dma((times - 1,)), dma((times - 1,)),
             dma((n - 1,)), dma((n - 1,)),
         ],

time: 47.1 us -> 47.7 us (1.013)
  Pallas kernels: 42.6 us -> 43.2 us
    pallas_call x1, Pallas kernels: 42.6 us -> 43.2 us  [shards(): pl.pallas_call(functools.partial(elementals_kernel, n, times, scale, corr...]
where the time goes in v5:
time: 47.7 us; the launch traced here: 47.5 us
  Pallas kernels  43.2 us (91%)
  local copies, waits for them, and re-layouts  2.99 us (6%)
  between operations  1.29 us (3%)
    pallas_call x1, Pallas kernels, shards(): pl.pallas_call(functools.partial(elementals_kernel, n, times, scale, corr...  43.2 us
    unnamed x3, local copies, waits for them, and re-layouts  2.35 us

profile of v5, /device:TPU:0, one launch (start us, length us, event | category | flops | bytes accessed | tf_op | source)
XLA Modules:
  0.0 47.5 jit_solution(3399010706774562830)
XLA Ops:
  1.3 43.2 %elementals.1 = (f32[8,64,128]{2,1,0:T(8,128)}, f32[4,2]{1,0:T(4,128)}) custom-call(f32[2,3,64,256]{3,2,1,0:T(8,128)} %bitcast.13, f32[16,64,128]{2,1,0:T(8,128)} %bitcast.12, s32[1]{0:T(128)S(6)} %copy.10.shift_ref, s32[4,3]{1,0:T(4,128)} %spin_ref.1), custom_call_target="tpu_custom_call" | custom-call | tf_op jit(solution)/shard_map/elementals/pallas_call | solution.py:400
  44.5 0.0 copy-start
  44.5 0.7 %copy-done = f32[4,2]{1,0:T(4,128)S(1)} copy-done((f32[4,2]{1,0:T(4,128)S(1)}, f32[4,2]{1,0:T(4,128)}, u32[]{:S(2)}) %copy-start) | copy-done | bytes 56
  45.2 0.6 %copy.8 = f32[4,2]{0,1:T(2,128)} copy(f32[4,2]{1,0:T(4,128)S(1)} %copy-done) | data formatting | bytes 64 | tf_op jit(solution)/shard_map/elementals/pallas_call | solution.py:400
  45.8 1.7 %copy.11 = f32[1,8,2,4096]{3,2,1,0:T(2,128)} copy(f32[1,8,2,4096]{3,2,1,0:T(2,128)} %bitcast.14) | data formatting | bytes 524288
Async XLA Ops:
  44.5 0.7 %copy-start = (f32[4,2]{1,0:T(4,128)S(1)}, f32[4,2]{1,0:T(4,128)}, u32[]{:S(2)}) copy-start(f32[4,2]{1,0:T(4,128)} %get-tuple-element.5) | copy-start | bytes 100
